TPU v7x, 32 devices: a whole 2x2x4 slice. The times are simulated.
32 devices in a mesh: blk: 8 (over y, x, core), cross: 4 (over z).
Axes of the slice: x: 2, y: 2, z: 4, core: 2. Of those that a mesh axis runs over, the one named last changes fastest.
Arguments:
- receiver_spectra: float32 [4096, 2, 1024], P(('blk', 'cross')), may hold values from -400 to 400
- source_spectra: float32 [4096, 2, 1024], P(('blk', 'cross')), may hold values from -400 to 400
- quality: int32 [4096], P(('blk', 'cross')), may hold values 0 or 1
- slot_order: int32 [32, 128], P(('blk', 'cross')), may hold values from 0 to 127, each once within a row
- owners: int32 [2, 8], replicated, may hold values from 0 to 3
Outputs:
- correlations: bfloat16 [2, 8, 4, 128, 128, 256], P(None, 'blk', 'cross')
Inputs may be any that keep to these rules, and one draw needn't show every extreme that they name: `slot_order`: each row is a permutation of 0 to 127.
All inputs are finite; a program needn't handle non-finite values. No bound on the sum of `quality` on one device may be relied on, other than what follows from the above.
Results may differ from a plain program's by a relative error of at most 0.0056.
Values sent between devices are 32-bit elements; how exact they have to be, the bound alone decides.
A program may use at most 128 MiB of HBM per device.

v0:
```python
import math
import jax
import jax.numpy as jnp
from jax import lax
from jax.sharding import PartitionSpec as P

L = 256
STEPS = 2


def passed_along(value, axis, steps):
    count = lax.axis_size(axis)
    pairs = [(source, (source + steps) % count) for source in range(count)]
    return lax.ppermute(value, axis, pairs)


def lag_tables(bins, lags):
    bin_index = jnp.arange(bins, dtype=jnp.int32)
    odd_index = 2 * jnp.arange(lags // 2, dtype=jnp.int32) + 1
    phase_turns = jnp.mod(bin_index[:, None] * odd_index[None, :], 4 * bins).astype(jnp.float32)
    phase_angle = phase_turns * (math.pi / (2 * bins))
    cos_table = (jnp.cos(phase_angle) / bins).astype(jnp.bfloat16)
    sin_table = (-jnp.sin(phase_angle) / bins).astype(jnp.bfloat16)
    return (cos_table, sin_table)


def whiten(spectra):
    mean_power = jnp.mean(spectra * spectra, axis=(1, 2), keepdims=True)
    return spectra * lax.rsqrt(mean_power + 1e-06)


def correlate(panel_spec, slab_spec, cos_table, sin_table):
    npanel = panel_spec.shape[0]
    nslab = slab_spec.shape[0]
    width = math.gcd(npanel, 16)
    blocks = panel_spec.reshape(npanel // width, width, 2, panel_spec.shape[2])

    def one_block(source):
        inphase = (
            source[:, None, 0, :] * slab_spec[None, :, 0, :]
            + source[:, None, 1, :] * slab_spec[None, :, 1, :]
        )
        quadrature = (
            source[:, None, 1, :] * slab_spec[None, :, 0, :]
            - source[:, None, 0, :] * slab_spec[None, :, 1, :]
        )
        inphase = inphase.astype(jnp.bfloat16).reshape(width * nslab, -1)
        quadrature = quadrature.astype(jnp.bfloat16).reshape(width * nslab, -1)
        even = jnp.dot(inphase, cos_table, preferred_element_type=jnp.float32)
        odd = jnp.dot(quadrature, sin_table, preferred_element_type=jnp.float32)
        joined = jnp.concatenate([even + odd, even - odd], axis=-1).astype(jnp.bfloat16)
        return joined.reshape(width, nslab, -1)

    lagged = lax.map(one_block, blocks)
    return lagged.reshape(npanel, nslab, lagged.shape[-1])


def local(receiver_spectra, source_spectra, quality, slot_order, owners):
    bins = receiver_spectra.shape[2]
    npanel = source_spectra.shape[0]
    cos_table, sin_table = lag_tables(bins, L)
    kept = quality.astype(jnp.float32)[:, None, None]
    receivers = whiten(receiver_spectra) * kept
    receivers = jnp.take(receivers, slot_order[0], axis=0)
    sources = whiten(source_spectra)
    block_index = lax.axis_index("blk")
    my_owners = lax.dynamic_index_in_dim(owners, block_index, 1, keepdims=False)
    every_panel = lax.all_gather(sources, "cross", axis=0, tiled=True)
    moving = receivers
    results = []
    for loop_step in range(STEPS):
        if loop_step > 0:
            moving = passed_along(moving, "blk", 1)
        owner_index = my_owners[loop_step]
        panel_spec = lax.dynamic_slice_in_dim(every_panel, owner_index * npanel, npanel, 0)
        results.append(correlate(panel_spec, moving, cos_table, sin_table))
    return jnp.stack(results)[:, None, None]


def solution(mesh):
    placed = (
        P(("blk", "cross"), None, None),
        P(("blk", "cross"), None, None),
        P(("blk", "cross")),
        P(("blk", "cross"), None),
        P(),
    )
    return jax.shard_map(
        local,
        mesh=mesh,
        in_specs=placed,
        out_specs=P(None, "blk", "cross", None, None, None),
        check_vma=False,
    )
```

profile of v0, /device:TPU:0, one launch (start us, length us, event | category | flops | bytes accessed | tf_op | source)
XLA Modules:
  0.0 305.8 jit_solution(16467009084390342149)
XLA Ops:
  21.7 73.5 %all-gather.2.cloned.1.call-done = f32[512,2,1024]{2,1,0:T(2,128)} async-done(((f32[128,2,1024]{2,1,0:T(2,128)}), f32[512,2,1024]{2,1,0:T(2,128)}) %all-gather.2.cloned.1.call-update) | async-done | bytes 4194320 | tf_op jit(solution)/shard_map/all_gather | solution.py:68
  95.1 3.2 %constant_dynamic-slice_fusion.1 = (f32[128,2,1024]{2,1,0:T(2,128)S(1)}, f32[128,2,1024]{2,1,0:T(2,128)}) fusion(f32[512,2,1024]{2,1,0:T(2,128)} %all-gather.2.cloned.1.call-done, s32[]{:T(128)S(6)} %select_n.44, s32[]{:T(128)S(6)} %select_n.49), kind=kLoop, calls=%fused_computation.86 | loop fusion | bytes 4194312 | tf_op jit(solution)/shard_map/dynamic_slice | solution.py:75
  98.4 4.3 %broadcast.91.clone = bf16[8,16,128,256]{3,2,1,0:T(8,128)(2,1)} broadcast(bf16[]{:T(256)} %constant.66.clone.1), dimensions={} | broadcast | bytes 8388610 | tf_op jit(solution)/shard_map/broadcast.6
  102.6 92.7 %while.25 = (s32[]{:T(128)}, bf16[8,16,128,256]{3,2,1,0:T(8,128)(2,1)}, f32[8,16,2,1024]{3,2,1,0:T(2,128)}, f32[128,2,1024]{2,1,0:T(2,128)S(1)}, s32[128]{0:T(128)S(1)}, /*index=5*/s32[]{:T(128)}) while((s32[]{:T(128)}, bf16[8,16,128,256]{3,2,1,0:T(8,128)(2,1)}, f32[8,16,2,1024]{3,2,1,0:T(2,128)}, ...), condition=%wide.region_5.6_spmd.clone.clone, body=%wide.region_4.5_spmd.clone.clone.sunk | while | flops 1097990144 | bytes 28181588 | solution.py:54
  104.7 2.7 subtract_convert_fusion.7
  107.4 2.9 fusion.81
  110.3 2.8 add_convert_fusion.7
  116.3 2.7 subtract_convert_fusion.7
  119.0 2.9 fusion.81
  121.9 2.8 add_convert_fusion.7
  127.9 2.7 subtract_convert_fusion.7
  130.6 2.9 fusion.81
  133.4 2.8 add_convert_fusion.7
  139.5 2.7 subtract_convert_fusion.7
  142.1 2.9 fusion.81
  145.0 2.8 add_convert_fusion.7
  151.1 2.7 subtract_convert_fusion.7
  153.7 2.9 fusion.81
  156.6 2.8 add_convert_fusion.7
  162.6 2.7 subtract_convert_fusion.7
  165.3 2.9 fusion.81
  168.2 2.8 add_convert_fusion.7
  174.2 2.7 subtract_convert_fusion.7
  176.9 2.9 fusion.81
  179.8 2.8 add_convert_fusion.7
  185.8 2.7 subtract_convert_fusion.7
  188.5 2.9 fusion.81
  191.4 2.8 add_convert_fusion.7
  195.4 4.3 %broadcast.91.clone.1 = bf16[8,16,128,256]{3,2,1,0:T(8,128)(2,1)} broadcast(bf16[]{:T(256)} %constant.66.clone.1), dimensions={} | broadcast | bytes 8388610 | tf_op jit(solution)/shard_map/broadcast.6
  199.7 85.5 %while.24 = (s32[]{:T(128)}, bf16[8,16,128,256]{3,2,1,0:T(8,128)(2,1)}, f32[8,16,2,1024]{3,2,1,0:T(2,128)S(1)}, f32[128,2,1024]{2,1,0:T(2,128)S(1)}, s32[128]{0:T(128)S(1)}, /*index=5*/s32[]{:T(128)}) while((s32[]{:T(128)}, bf16[8,16,128,256]{3,2,1,0:T(8,128)(2,1)}, f32[8,16,2,1024]{3,2,1,0:T(2,128)S(1)}, ...), condition=%wide.region_3.4_spmd.clone.clone, body=%wide.region_2.3_spmd.clone.clone.sunk | while | flops 1097990144 | bytes 28181588 | solution.py:54
  200.8 2.7 subtract_convert_fusion.6
  203.5 2.9 fusion.76
  206.4 2.8 add_convert_fusion.6
  214.3 2.9 fusion.76
  217.1 2.8 add_convert_fusion.6
  224.9 2.9 fusion.76
  227.8 2.8 add_convert_fusion.6
  235.6 2.9 fusion.76
  238.5 2.8 add_convert_fusion.6
  246.3 2.9 fusion.76
  249.2 2.8 add_convert_fusion.6
  257.0 2.9 fusion.76
  259.9 2.8 add_convert_fusion.6
  267.7 2.9 fusion.76
  270.5 2.8 add_convert_fusion.6
  278.4 2.9 fusion.76
  281.2 2.8 add_convert_fusion.6
  285.2 13.8 %maximum_bitcast_fusion = bf16[2,1,1,128,128,256]{5,4,3,2,1,0:T(8,128)(2,1)} fusion(bf16[1,128,128,256]{3,2,1,0:T(8,128)(2,1)} %bitcast.87, bf16[1,128,128,256]{3,2,1,0:T(8,128)(2,1)} %bitcast.86), kind=kLoop, calls=%fused_computation.75 | loop fusion | flops 8388608 | bytes 33554432 | tf_op jit(solution)/shard_map/broadcast_in_dim | solution.py:77
  (128 shorter events, 76.5 us)
Async XLA Ops:
  6.5 13.2 %copy-start = (s32[2,8]{1,0:T(2,128)S(1)}, s32[2,8]{1,0:T(2,128)}, u32[]{:S(2)}) copy-start(s32[2,8]{1,0:T(2,128)} %param.13) | copy-start | bytes 196
  6.5 11.9 %copy-start.2 = (s32[1,128]{1,0:T(1,128)S(1)}, s32[1,128]{1,0:T(1,128)}, u32[]{:S(2)}) copy-start(s32[1,128]{1,0:T(1,128)} %param.12) | copy-start | bytes 1540
  6.5 88.6 %all-gather.2.cloned.1.call-start = ((), (), s32[]{:S(2)}) async-start(), calls=%async_computation | async-start | bytes 5242880 | tf_op jit(solution)/shard_map/all_gather | solution.py:68
  19.0 79.3 %collective-permute-start = (f32[128,2,1024]{2,1,0:T(2,128)S(1)}, f32[128,2,1024]{2,1,0:T(2,128)S(1)}, u32[]{:S(2)}, u32[]{:S(2)}) collective-permute-start(f32[128,2,1024]{2,1,0:T(2,128)S(1)} %broadcast_select_fusion), channel_id=1, source_target_pairs={{0,4},{4,8},{8,12},{12,16},{16,20},{20,24},{24,28},{28,0},{1,5},{5... | collective-permute-start | bytes 3145736 | tf_op jit(solution)/shard_map/ppermute | solution.py:14
  285.2 13.8 %copy-start.1 = (s32[2,8]{1,0:T(2,128)S(1)}, s32[2,8]{1,0:T(2,128)}, u32[]{:S(2)}) copy-start(s32[2,8]{1,0:T(2,128)} %param.13) | copy-start | bytes 196
Sparse Core Ops, SparseCore 0:
  11.6 83.4 all-gather.1
where the time goes:
time: 306 us
  matrix products  90.8 us (30%)
  other arithmetic  85.6 us (28%)
  waiting for transfers between devices  73.5 us (24%)
  local copies, waits for them, and re-layouts  39.7 us (13%)
  between operations  14.7 us (5%)
    all_gather x1, waiting for transfers between devices, local(): every_panel = lax.all_gather(sources, 'cross', axis=0, tiled=True)  73.5 us
    dot_general x16, matrix products, one_block(): odd = jnp.dot(quadrature, sin_table, preferred_element_type=jnp.float32)  45.8 us
    dot_general x16, matrix products, one_block(): even = jnp.dot(inphase, cos_table, preferred_element_type=jnp.float32)  45 us
    convert_element_type x16, other arithmetic, one_block(): quadrature = quadrature.astype(jnp.bfloat16).reshape(width * nslab, -1)  42.7 us
    dynamic_update_slice x16, other arithmetic, correlate(): lagged = lax.map(one_block, blocks)  18.4 us
    broadcast_in_dim x1, other arithmetic, local(): return jnp.stack(results)[:, None, None]  13.8 us
    slice x16, local copies, waits for them, and re-layouts, one_block(): slab_spec[None, :, 0, :]  13 us
    another operation x2, local copies, waits for them, and re-layouts  8.57 us
  transfers between devices with their start and end apart: 2, of which 1 were waited for; matrix products, arithmetic and copies ran while one was open for 4% of the time, Pallas kernels for 0%

commit v1 on v0

--- a/solution.py
+++ b/solution.py
@@ -6,6 +6,22 @@
 
 L = 256
 STEPS = 2
+
+
+def _cut_task(inp, join_dim):
+    n = jax.lax.psum(1, "cross")
+    block_now = range(n)
+    taken_in = map(lambda pp: (pp, (pp + 1) % n), block_now)
+    blocks_here = list(taken_in)
+    f_now = [None] * n
+    f_now[n - 1] = inp
+    for q in range(n - 2, -1, -1):
+        f_now[q] = jax.lax.ppermute(f_now[q + 1], "cross", blocks_here)
+    newest = jnp.concatenate(f_now, join_dim)
+    after = jax.lax.axis_index("cross")
+    w2 = (after + 1) * inp.shape[join_dim]
+    next_value = jnp.roll(newest, w2, join_dim)
+    return next_value
 
 
 def passed_along(value, axis, steps):
@@ -65,7 +81,7 @@
     sources = whiten(source_spectra)
     block_index = lax.axis_index("blk")
     my_owners = lax.dynamic_index_in_dim(owners, block_index, 1, keepdims=False)
-    every_panel = lax.all_gather(sources, "cross", axis=0, tiled=True)
+    every_panel = _cut_task(sources, 0)
     moving = receivers
     results = []
     for loop_step in range(STEPS):

time: 306 us -> 295 us (0.964)
  between operations: 14.7 us -> 1.37 us
  waiting for transfers between devices: 73.5 us -> 65.1 us
  local copies, waits for them, and re-layouts: 39.7 us -> 46.3 us
    all_gather x1 -> x0, waiting for transfers between devices: 73.5 us -> none  [local(): every_panel = lax.all_gather(sources, 'cross', axis=0, tiled=True)]
    ppermute x0 -> x3, waiting for transfers between devices: none -> 65.1 us  [_cut_task(): f_now[q] = jax.lax.ppermute(f_now[q + 1], 'cross', blocks_here)]
    unnamed x6 -> x18, local copies, waits for them, and re-layouts: 0.01 us -> 6.9 us
    ppermute x0 -> x3, starting transfers between devices: none -> 3.11 us  [_cut_task(): f_now[q] = jax.lax.ppermute(f_now[q + 1], 'cross', blocks_here)]
  transfers between devices with their start and end apart: 2 -> 4, of which waited for: 1 -> 3; matrix products, arithmetic and copies ran while one was open for 4% -> 7% of each run, Pallas kernels for 0% -> 0%
where the time goes in v1:
time: 295 us
  matrix products  90.8 us (31%)
  other arithmetic  86.8 us (29%)
  waiting for transfers between devices  65.1 us (22%)
  local copies, waits for them, and re-layouts  46.3 us (16%)
  starting transfers between devices  3.35 us (1%)
    ppermute x3, waiting for transfers between devices, _cut_task(): f_now[q] = jax.lax.ppermute(f_now[q + 1], 'cross', blocks_here)  65.1 us
    dot_general x16, matrix products, one_block(): odd = jnp.dot(quadrature, sin_table, preferred_element_type=jnp.float32)  45.8 us
    dot_general x16, matrix products, one_block(): even = jnp.dot(inphase, cos_table, preferred_element_type=jnp.float32)  45 us
    convert_element_type x16, other arithmetic, one_block(): quadrature = quadrature.astype(jnp.bfloat16).reshape(width * nslab, -1)  42.7 us
    dynamic_update_slice x16, other arithmetic, correlate(): lagged = lax.map(one_block, blocks)  18.4 us
    broadcast_in_dim x1, other arithmetic, local(): return jnp.stack(results)[:, None, None]  13.8 us
    slice x16, local copies, waits for them, and re-layouts, one_block(): slab_spec[None, :, 0, :]  13 us
    another operation x2, local copies, waits for them, and re-layouts  8.56 us
  transfers between devices with their start and end apart: 4, of which 3 were waited for; matrix products, arithmetic and copies ran while one was open for 7% of the time, Pallas kernels for 0%

profile of v1, /device:TPU:0, one launch (start us, length us, event | category | flops | bytes accessed | tf_op | source)
XLA Modules:
  0.0 294.5 jit_solution(1800164442833819478)
XLA Ops:
  4.0 3.1 %collective-permute-start = (f32[128,2,1024]{2,1,0:T(2,128)S(1)}, f32[128,2,1024]{2,1,0:T(2,128)S(1)}, u32[]{:S(2)}, u32[]{:S(2)}) collective-permute-start(f32[128,2,1024]{2,1,0:T(2,128)S(1)} %broadcast_multiply_fusion), channel_id=1, source_target_pairs={{0,1},{1,2},{2,3},{3,0},{4,5},{5,6},{6,7},{7,4},{8,9},{9,10},{10,1... | collective-permute-start | bytes 3145736 | tf_op jit(solution)/shard_map/ppermute | solution.py:19
  7.1 25.2 %collective-permute-done = f32[128,2,1024]{2,1,0:T(2,128)S(1)} collective-permute-done((f32[128,2,1024]{2,1,0:T(2,128)S(1)}, f32[128,2,1024]{2,1,0:T(2,128)S(1)}, u32[]{:S(2)}, u32[]{:S(2)}) %collective-permute-start) | collective-permute-done | bytes 1048608 | tf_op jit(solution)/shard_map/ppermute | solution.py:19
  35.9 22.6 %collective-permute-done.1 = f32[128,2,1024]{2,1,0:T(2,128)} collective-permute-done((f32[128,2,1024]{2,1,0:T(2,128)S(1)}, f32[128,2,1024]{2,1,0:T(2,128)}, u32[]{:S(2)}, u32[]{:S(2)}) %collective-permute-start.1) | collective-permute-done | bytes 1048608 | tf_op jit(solution)/shard_map/ppermute | solution.py:19
  58.6 2.7 multiply_multiply_fusion
  61.2 2.9 gather_fusion
  66.8 17.3 %collective-permute-done.2 = f32[128,2,1024]{2,1,0:T(2,128)} collective-permute-done((f32[128,2,1024]{2,1,0:T(2,128)}, f32[128,2,1024]{2,1,0:T(2,128)}, u32[]{:S(2)}, u32[]{:S(2)}) %collective-permute-start.2) | collective-permute-done | bytes 1048608 | tf_op jit(solution)/shard_map/ppermute | solution.py:19
  93.9 4.3 %broadcast.92.clone = bf16[8,16,128,256]{3,2,1,0:T(8,128)(2,1)} broadcast(bf16[]{:T(256)} %constant.113.clone.1), dimensions={} | broadcast | bytes 8388610 | tf_op jit(solution)/shard_map/broadcast.6
  98.1 92.7 %while.25 = (s32[]{:T(128)}, bf16[8,16,128,256]{3,2,1,0:T(8,128)(2,1)}, f32[8,16,2,1024]{3,2,1,0:T(2,128)}, f32[128,2,1024]{2,1,0:T(2,128)S(1)}, s32[128]{0:T(128)S(1)}, /*index=5*/s32[]{:T(128)}) while((s32[]{:T(128)}, bf16[8,16,128,256]{3,2,1,0:T(8,128)(2,1)}, f32[8,16,2,1024]{3,2,1,0:T(2,128)}, ...), condition=%wide.region_5.6_spmd.clone.clone, body=%wide.region_4.5_spmd.clone.clone.sunk | while | flops 1097990144 | bytes 28181588 | solution.py:70
  100.2 2.7 subtract_convert_fusion.7
  102.9 2.9 fusion.81
  105.8 2.8 add_convert_fusion.7
  111.8 2.7 subtract_convert_fusion.7
  114.5 2.9 fusion.81
  117.4 2.8 add_convert_fusion.7
  123.4 2.7 subtract_convert_fusion.7
  126.1 2.9 fusion.81
  128.9 2.8 add_convert_fusion.7
  135.0 2.7 subtract_convert_fusion.7
  137.6 2.9 fusion.81
  140.5 2.8 add_convert_fusion.7
  146.5 2.7 subtract_convert_fusion.7
  149.2 2.9 fusion.81
  152.1 2.8 add_convert_fusion.7
  160.8 2.9 fusion.81
  163.7 2.8 add_convert_fusion.7
  172.4 2.9 fusion.81
  175.2 2.8 add_convert_fusion.7
  184.0 2.9 fusion.81
  186.8 2.8 add_convert_fusion.7
  190.8 4.3 %broadcast.92.clone.1 = bf16[8,16,128,256]{3,2,1,0:T(8,128)(2,1)} broadcast(bf16[]{:T(256)} %constant.113.clone.1), dimensions={} | broadcast | bytes 8388610 | tf_op jit(solution)/shard_map/broadcast.6
  195.1 85.6 %while.24 = (s32[]{:T(128)}, bf16[8,16,128,256]{3,2,1,0:T(8,128)(2,1)}, f32[8,16,2,1024]{3,2,1,0:T(2,128)S(1)}, f32[128,2,1024]{2,1,0:T(2,128)S(1)}, s32[128]{0:T(128)S(1)}, /*index=5*/s32[]{:T(128)}) while((s32[]{:T(128)}, bf16[8,16,128,256]{3,2,1,0:T(8,128)(2,1)}, f32[8,16,2,1024]{3,2,1,0:T(2,128)S(1)}, ...), condition=%wide.region_3.4_spmd.clone.clone, body=%wide.region_2.3_spmd.clone.clone.sunk | while | flops 1097990144 | bytes 28181588 | solution.py:70
  199.0 2.9 fusion.76
  201.8 2.8 add_convert_fusion.6
  209.7 2.9 fusion.76
  212.6 2.8 add_convert_fusion.6
  220.4 2.9 fusion.76
  223.3 2.8 add_convert_fusion.6
  231.1 2.9 fusion.76
  234.0 2.8 add_convert_fusion.6
  241.8 2.9 fusion.76
  244.7 2.8 add_convert_fusion.6
  252.5 2.9 fusion.76
  255.4 2.8 add_convert_fusion.6
  263.2 2.9 fusion.76
  266.1 2.8 add_convert_fusion.6
  273.9 2.9 fusion.76
  276.7 2.8 add_convert_fusion.6
  280.7 13.8 %maximum_bitcast_fusion = bf16[2,1,1,128,128,256]{5,4,3,2,1,0:T(8,128)(2,1)} fusion(bf16[1,128,128,256]{3,2,1,0:T(8,128)(2,1)} %bitcast.87, bf16[1,128,128,256]{3,2,1,0:T(8,128)(2,1)} %bitcast.86), kind=kLoop, calls=%fused_computation.75 | loop fusion | flops 8388608 | bytes 33554432 | tf_op jit(solution)/shard_map/broadcast_in_dim | solution.py:93
  (145 shorter events, 92.0 us)
Async XLA Ops:
  0.0 65.0 %copy-start = (s32[2,8]{1,0:T(2,128)S(1)}, s32[2,8]{1,0:T(2,128)}, u32[]{:S(2)}) copy-start(s32[2,8]{1,0:T(2,128)} %param.13) | copy-start | bytes 196
  0.0 88.2 %copy-start.2 = (f32[128,2,1024]{2,1,0:T(2,128)S(1)}, f32[128,2,1024]{2,1,0:T(2,128)}, u32[]{:S(2)}) copy-start(f32[128,2,1024]{2,1,0:T(2,128)} %param.10) | copy-start | bytes 3145732
  0.0 64.2 %copy-start.5 = (s32[1,128]{1,0:T(1,128)S(1)}, s32[1,128]{1,0:T(1,128)}, u32[]{:S(2)}) copy-start(s32[1,128]{1,0:T(1,128)} %param.12) | copy-start | bytes 1540
  4.0 28.3 %collective-permute-start = (f32[128,2,1024]{2,1,0:T(2,128)S(1)}, f32[128,2,1024]{2,1,0:T(2,128)S(1)}, u32[]{:S(2)}, u32[]{:S(2)}) collective-permute-start(f32[128,2,1024]{2,1,0:T(2,128)S(1)} %broadcast_multiply_fusion), channel_id=1, source_target_pairs={{0,1},{1,2},{2,3},{3,0},{4,5},{5,6},{6,7},{7,4},{8,9},{9,10},{10,1... | collective-permute-start | bytes 3145736 | tf_op jit(solution)/shard_map/ppermute | solution.py:19
  32.3 31.8 %copy-start.3 = (f32[128,2,1024]{2,1,0:T(2,128)}, f32[128,2,1024]{2,1,0:T(2,128)S(1)}, u32[]{:S(2)}) copy-start(f32[128,2,1024]{2,1,0:T(2,128)S(1)} %collective-permute-done) | copy-start | bytes 3145732
  32.3 26.2 %collective-permute-start.1 = (f32[128,2,1024]{2,1,0:T(2,128)S(1)}, f32[128,2,1024]{2,1,0:T(2,128)}, u32[]{:S(2)}, u32[]{:S(2)}) collective-permute-start(f32[128,2,1024]{2,1,0:T(2,128)S(1)} %collective-permute-done), channel_id=1, source_target_pairs={{0,1},{1,2},{2,3},{3,0},{4,5},{5,6},{6,7},{7,4},{8,9},{9,10},{10,1... | collective-permute-start | bytes 3145736 | tf_op jit(solution)/shard_map/ppermute | solution.py:19
  58.6 25.6 %collective-permute-start.2 = (f32[128,2,1024]{2,1,0:T(2,128)}, f32[128,2,1024]{2,1,0:T(2,128)}, u32[]{:S(2)}, u32[]{:S(2)}) collective-permute-start(f32[128,2,1024]{2,1,0:T(2,128)} %collective-permute-done.1), channel_id=1, source_target_pairs={{0,1},{1,2},{2,3},{3,0},{4,5},{5,6},{6,7},{7,4},{8,9},{9,10},{10,1... | collective-permute-start | bytes 3145736 | tf_op jit(solution)/shard_map/ppermute | solution.py:19
  64.7 29.1 %collective-permute-start.3 = (f32[128,2,1024]{2,1,0:T(2,128)S(1)}, f32[128,2,1024]{2,1,0:T(2,128)S(1)}, u32[]{:S(2)}, u32[]{:S(2)}) collective-permute-start(f32[128,2,1024]{2,1,0:T(2,128)S(1)} %broadcast_select_fusion), channel_id=1, source_target_pairs={{0,4},{4,8},{8,12},{12,16},{16,20},{20,24},{24,28},{28,0},{1,5},{5... | collective-permute-start | bytes 3145736 | tf_op jit(solution)/shard_map/ppermute | solution.py:30
  66.8 24.6 %copy-start.4 = (f32[128,2,1024]{2,1,0:T(2,128)S(1)}, f32[128,2,1024]{2,1,0:T(2,128)}, u32[]{:S(2)}) copy-start(f32[128,2,1024]{2,1,0:T(2,128)} %copy-done.3) | copy-start | bytes 3145732
  280.7 13.8 %copy-start.1 = (s32[2,8]{1,0:T(2,128)S(1)}, s32[2,8]{1,0:T(2,128)}, u32[]{:S(2)}) copy-start(s32[2,8]{1,0:T(2,128)} %param.13) | copy-start | bytes 196
